TPU v7x, 32 devices: a whole 2x2x4 slice. The times are simulated.
32 devices in a mesh: groups: 2 (over y), req: 2 (over core), ctx: 8 (over z, x).
Axes of the slice: x: 2, y: 2, z: 4, core: 2. Of those that a mesh axis runs over, the one named last changes fastest.
Arguments:
- queries: bfloat16 [4, 1024, 4096], P(('groups', 'req'), 'ctx'), parts along dimension 0, may hold values from -6 to 6
- keys: bfloat16 [4, 1024, 512], P(('groups', 'req'), 'ctx'), parts along dimension 0, may hold values from -6 to 6
- values: bfloat16 [4, 1024, 512], P(('groups', 'req'), 'ctx'), parts along dimension 0, may hold values from -6 to 6
- cache_keys: bfloat16 [16, 256, 512], P(('groups', 'ctx')), parts along dimension 0, may hold values from -6 to 6
- cache_values: bfloat16 [16, 256, 512], P(('groups', 'ctx')), parts along dimension 0, may hold values from -6 to 6
- doc_lengths: int32 [4], P('groups'), parts along dimension 0, may hold values from 32 to 256, as said below
- doc_owners: int32 [4], P('groups'), parts along dimension 0, may hold values from 0 to 7, as said below
- block_offsets: int32 [4], P('groups'), parts along dimension 0, may hold values from 1 to 7
Outputs:
- attended: bfloat16 [4, 1024, 4096], P(('groups', 'req'), 'ctx'), parts along dimension 0
There are 2 independent parts, one for each index of `groups`. A program takes and returns all parts, laid end to end along the dimension named above; each array names one. Nothing has to cross between parts.
Inputs may be any that keep to these rules, and one draw needn't show every extreme that they name: `doc_lengths`: one document block has exactly 256 live rows. `doc_owners`: the owners of the two document blocks differ.
All inputs are finite; a program needn't handle non-finite values.
Results may differ from a plain program's by a relative error of at most 0.0065.
Values may be sent and summed in bfloat16 or wider, within the bound.
No kernel may reach another device: no remote copies, remote signals or barrier semaphores. Data moves between devices by JAX's collectives and lax.ppermute only.
A program may use at most 64 MiB of HBM per device.

v0:
```python
import math
import jax
import jax.numpy as jnp
from jax import lax
from jax.sharding import PartitionSpec as P

HD = 128
HOPS = 3
NEGATIVE = -1e30


def broadcast(block, axis, source):
    block = jnp.where(lax.axis_index(axis) == source, block, jnp.zeros_like(block))
    return lax.psum(block, axis)


def from_behind(value, axis, steps):
    count = lax.axis_size(axis)
    pairs = [(source, (source + steps) % count) for source in range(count)]
    return lax.ppermute(value, axis, pairs)


def merge_block(carried, query_rows, key_rows, value_rows, allowed):
    running, totals, summed = carried
    scores = jnp.einsum(
        "tid,sd->its", query_rows, key_rows, preferred_element_type=jnp.float32
    ) / math.sqrt(HD)
    scores = jnp.where(allowed[None], scores, NEGATIVE)
    highest = jnp.maximum(running, jnp.max(scores, axis=-1))
    weights = jnp.where(allowed[None], jnp.exp(scores - highest[..., None]), 0.0)
    shrink = jnp.exp(running - highest)
    totals = totals * shrink + jnp.sum(weights, axis=-1)
    summed = summed * shrink[..., None] + jnp.einsum(
        "its,sd->itd", weights.astype(jnp.bfloat16), value_rows, preferred_element_type=jnp.float32
    )
    return (highest, totals, summed)


def per_device(
    queries, keys, values, cache_keys, cache_values, doc_lengths, doc_owners, block_offsets
):
    cycle_size = lax.axis_size("ctx")
    position = lax.axis_index("ctx")
    request = lax.axis_index("req")
    tokens = queries.shape[1]
    kv_width = keys.shape[2]
    kv_heads = kv_width // HD
    group_size = queries.shape[2] // kv_width
    doc_rows = cache_keys.shape[1]
    offset = jnp.sum(jnp.where(jnp.arange(block_offsets.shape[0]) == request, block_offsets, 0))
    placed = (position - offset) % cycle_size
    inside = jnp.arange(tokens)
    resident = jnp.stack([keys[0], values[0]])
    blocks = [(resident, inside[None, :] <= inside[:, None])]
    cached = jnp.stack([cache_keys[0], cache_values[0]])
    doc_pairs = [broadcast(cached, "ctx", doc_owners[number]) for number in range(2)]
    for number in range(2):
        doc_live = jnp.broadcast_to(
            jnp.arange(doc_rows)[None, :] < doc_lengths[number], (tokens, doc_rows)
        )
        blocks.append((doc_pairs[number], doc_live))
    moving = resident
    for hop_count in range(1, HOPS + 1):
        moving = from_behind(moving, "ctx", 1)
        blocks.append((moving, jnp.broadcast_to(placed >= hop_count, (tokens, tokens))))
    query_heads = queries[0].reshape(tokens, kv_heads, group_size, HD)
    outputs = []
    for head_index in range(kv_heads):
        columns = slice(head_index * HD, (head_index + 1) * HD)
        query_rows = query_heads[:, head_index]
        carried = (
            jnp.full((group_size, tokens), NEGATIVE, jnp.float32),
            jnp.zeros((group_size, tokens), jnp.float32),
            jnp.zeros((group_size, tokens, HD), jnp.float32),
        )
        for paired, allowed in blocks:
            carried = merge_block(
                carried, query_rows, paired[0][:, columns], paired[1][:, columns], allowed
            )
        outputs.append(jnp.transpose(carried[2] / carried[1][..., None], (1, 0, 2)))
    attended = jnp.stack(outputs, axis=1).reshape(tokens, kv_heads * group_size * HD)
    return attended.astype(jnp.bfloat16)[None]


def solution(mesh):
    return jax.shard_map(
        per_device,
        mesh=mesh,
        in_specs=(
            P(("groups", "req"), "ctx", None),
            P(("groups", "req"), "ctx", None),
            P(("groups", "req"), "ctx", None),
            P(("groups", "ctx"), None, None),
            P(("groups", "ctx"), None, None),
            P("groups"),
            P("groups"),
            P("groups"),
        ),
        out_specs=P(("groups", "req"), "ctx", None),
        check_vma=False,
    )
```

profile of v0, /device:TPU:0, one launch (start us, length us, event | category | flops | bytes accessed | tf_op | source)
XLA Modules:
  0.0 129.9 jit_solution(4399630337771953146)
XLA Ops:
  6.5 1.0 pad_maximum_fusion.1
  7.6 3.0 %collective-permute-start = (bf16[2,128,512]{2,1,0:T(8,128)(2,1)S(1)}, bf16[2,128,512]{2,1,0:T(8,128)(2,1)S(1)}, u32[]{:S(2)}, u32[]{:S(2)}) collective-permute-start(bf16[2,128,512]{2,1,0:T(8,128)(2,1)S(1)} %pad_maximum_fusion.1), channel_id=1, source_target_pairs={{0,1},{1,2},{2,3},{3,4},{4,5},{5,6},{6,7},{7,0},{8,9},{9,10},{10,1... | collective-permute-start | bytes 786440 | tf_op jit(solution)/shard_map/ppermute | solution.py:20
  10.6 0.7 copy-done.36
  11.3 0.7 fusion.326
  13.3 0.9 copy-done.16
  14.3 1.1 broadcast_select_fusion.1
  15.4 0.5 copy-done.12
  15.9 0.7 copy.55
  16.8 1.6 %fusion.350 = (f32[8,128]{1,0:T(8,128)}, f32[8,128,128]{1,2,0:T(8,128)}) fusion(bf16[128,4,8,128]{0,3,2,1:T(8,128)(2,1)S(1)} %bitcast.900, bf16[128,512]{1,0:T(8,128)(2,1)S(1)} %bitcast.929, pred[128,128]{0,1:T(8,128)(4,1)S(1)} %iota_compare_fusion), kind=kOutput, calls=%fused_computation.530 | convolution fusion | flops 33946624 | bytes 839680 | tf_op jit(solution)/shard_map/tid,sd->its/dot_general | solution.py:25
  18.4 1.6 %fusion.344 = (f32[8,128]{1,0:T(8,128)}, f32[8,128,128]{1,2,0:T(8,128)}) fusion(bf16[128,4,8,128]{0,3,2,1:T(8,128)(2,1)S(1)} %bitcast.901, bf16[128,512]{1,0:T(8,128)(2,1)S(1)} %bitcast.930, pred[128,128]{0,1:T(8,128)(4,1)S(1)} %iota_compare_fusion), kind=kOutput, calls=%fused_computation.524 | convolution fusion | flops 33946624 | bytes 839680 | tf_op jit(solution)/shard_map/tid,sd->its/dot_general | solution.py:25
  20.0 1.6 %fusion.338 = (f32[8,128]{1,0:T(8,128)}, f32[8,128,128]{1,2,0:T(8,128)}) fusion(bf16[128,4,8,128]{0,3,2,1:T(8,128)(2,1)S(1)} %bitcast.902, bf16[128,512]{1,0:T(8,128)(2,1)S(1)} %bitcast.931, pred[128,128]{0,1:T(8,128)(4,1)S(1)} %iota_compare_fusion), kind=kOutput, calls=%fused_computation.518 | convolution fusion | flops 33946624 | bytes 839680 | tf_op jit(solution)/shard_map/tid,sd->its/dot_general | solution.py:25
  21.6 0.7 copy-done.37
  22.3 0.6 fusion.325
  22.9 1.2 iota_compare_fusion.1
  24.1 0.7 fusion.284
  24.8 1.2 iota_compare_fusion.2
  26.9 1.6 %fusion.332 = (f32[8,128]{1,0:T(8,128)}, f32[8,128,128]{1,2,0:T(8,128)}) fusion(bf16[128,4,8,128]{0,3,2,1:T(8,128)(2,1)S(1)} %bitcast.903, bf16[128,512]{1,0:T(8,128)(2,1)S(1)} %bitcast.932, pred[128,128]{0,1:T(8,128)(4,1)S(1)} %iota_compare_fusion), kind=kOutput, calls=%fused_computation.512 | convolution fusion | flops 33946624 | bytes 839680 | tf_op jit(solution)/shard_map/tid,sd->its/dot_general | solution.py:25
  28.5 0.8 fusion.347
  29.3 1.6 %fusion.341 = (f32[8,128]{1,0:T(8,128)}, f32[8,128,128]{1,2,0:T(8,128)}) fusion(bf16[128,4,8,128]{0,3,2,1:T(8,128)(2,1)S(1)} %bitcast.905, bf16[128,512]{1,0:T(8,128)(2,1)S(1)} %get-tuple-element.70, pred[]{:T(512)S(6)} %ge.9), kind=kOutput, calls=%fused_computation.521 | convolution fusion | flops 33946624 | bytes 823297 | tf_op jit(solution)/shard_map/tid,sd->its/dot_general | solution.py:25
  30.9 1.5 %collective-permute-start.1 = (bf16[2,128,512]{2,1,0:T(8,128)(2,1)S(1)}, bf16[2,128,512]{2,1,0:T(8,128)(2,1)S(1)}, u32[]{:S(2)}, u32[]{:S(2)}) collective-permute-start(bf16[2,128,512]{2,1,0:T(8,128)(2,1)S(1)} %collective-permute-done), channel_id=1, source_target_pairs={{0,1},{1,2},{2,3},{3,4},{4,5},{5,6},{6,7},{7,0},{8,9},{9,10},{10,1... | collective-permute-start | bytes 786440 | tf_op jit(solution)/shard_map/ppermute | solution.py:20
  32.5 1.6 %fusion.335 = (f32[8,128]{1,0:T(8,128)}, f32[8,128,128]{1,2,0:T(8,128)}) fusion(bf16[128,4,8,128]{0,3,2,1:T(8,128)(2,1)S(1)} %bitcast.906, bf16[128,512]{1,0:T(8,128)(2,1)S(1)} %get-tuple-element.70, pred[]{:T(512)S(6)} %ge.9), kind=kOutput, calls=%fused_computation.515 | convolution fusion | flops 33946624 | bytes 823297 | tf_op jit(solution)/shard_map/tid,sd->its/dot_general | solution.py:25
  34.1 0.8 fusion.329
  34.9 8.0 %collective-permute-done.1 = bf16[2,128,512]{2,1,0:T(8,128)(2,1)S(1)} collective-permute-done((bf16[2,128,512]{2,1,0:T(8,128)(2,1)S(1)}, bf16[2,128,512]{2,1,0:T(8,128)(2,1)S(1)}, u32[]{:S(2)}, u32[]{:S(2)}) %collective-permute-start.1) | collective-permute-done | bytes 262176 | tf_op jit(solution)/shard_map/ppermute | solution.py:20
  43.0 0.8 fusion.346
  43.8 1.6 %fusion.340 = (f32[8,128]{1,0:T(8,128)}, f32[8,128,128]{1,2,0:T(8,128)}) fusion(bf16[128,4,8,128]{0,3,2,1:T(8,128)(2,1)S(1)} %bitcast.909, bf16[128,512]{1,0:T(8,128)(2,1)S(1)} %get-tuple-element.68, pred[]{:T(512)S(6)} %ge.10), kind=kOutput, calls=%fused_computation.520 | convolution fusion | flops 33946624 | bytes 823297 | tf_op jit(solution)/shard_map/tid,sd->its/dot_general | solution.py:25
  45.4 1.6 %fusion.334 = (f32[8,128]{1,0:T(8,128)}, f32[8,128,128]{1,2,0:T(8,128)}) fusion(bf16[128,4,8,128]{0,3,2,1:T(8,128)(2,1)S(1)} %bitcast.910, bf16[128,512]{1,0:T(8,128)(2,1)S(1)} %get-tuple-element.68, pred[]{:T(512)S(6)} %ge.10), kind=kOutput, calls=%fused_computation.514 | convolution fusion | flops 33946624 | bytes 823297 | tf_op jit(solution)/shard_map/tid,sd->its/dot_general | solution.py:25
  47.0 0.8 fusion.328
  47.9 10.0 %collective-permute-done.2 = bf16[2,128,512]{2,1,0:T(8,128)(2,1)S(1)} collective-permute-done((bf16[2,128,512]{2,1,0:T(8,128)(2,1)S(1)}, bf16[2,128,512]{2,1,0:T(8,128)(2,1)S(1)}, u32[]{:S(2)}, u32[]{:S(2)}) %collective-permute-start.2) | collective-permute-done | bytes 262176 | tf_op jit(solution)/shard_map/ppermute | solution.py:20
  57.9 0.7 slice_bitcast_fusion.8
  58.5 1.6 %fusion.345 = (f32[8,128]{1,0:T(8,128)}, f32[8,128,128]{1,2,0:T(8,128)}) fusion(bf16[128,4,8,128]{0,3,2,1:T(8,128)(2,1)S(1)} %bitcast.912, bf16[128,512]{1,0:T(8,128)(2,1)S(1)} %get-tuple-element.66, pred[]{:T(512)S(6)} %ge.11), kind=kOutput, calls=%fused_computation.525 | convolution fusion | flops 33946624 | bytes 823297 | tf_op jit(solution)/shard_map/tid,sd->its/dot_general | solution.py:25
  60.2 1.6 %fusion.339 = (f32[8,128]{1,0:T(8,128)}, f32[8,128,128]{1,2,0:T(8,128)}) fusion(bf16[128,4,8,128]{0,3,2,1:T(8,128)(2,1)S(1)} %bitcast.913, bf16[128,512]{1,0:T(8,128)(2,1)S(1)} %get-tuple-element.66, pred[]{:T(512)S(6)} %ge.11), kind=kOutput, calls=%fused_computation.519 | convolution fusion | flops 33946624 | bytes 823297 | tf_op jit(solution)/shard_map/tid,sd->its/dot_general | solution.py:25
  61.8 1.6 %fusion.333 = (f32[8,128]{1,0:T(8,128)}, f32[8,128,128]{1,2,0:T(8,128)}) fusion(bf16[128,4,8,128]{0,3,2,1:T(8,128)(2,1)S(1)} %bitcast.914, bf16[128,512]{1,0:T(8,128)(2,1)S(1)} %get-tuple-element.66, pred[]{:T(512)S(6)} %ge.11), kind=kOutput, calls=%fused_computation.513 | convolution fusion | flops 33946624 | bytes 823297 | tf_op jit(solution)/shard_map/tid,sd->its/dot_general | solution.py:25
  63.4 1.6 %fusion.327 = (f32[8,128]{1,0:T(8,128)}, f32[8,128,128]{1,2,0:T(8,128)}) fusion(bf16[128,4,8,128]{0,3,2,1:T(8,128)(2,1)S(1)} %bitcast.915, bf16[128,512]{1,0:T(8,128)(2,1)S(1)} %get-tuple-element.66, pred[]{:T(512)S(6)} %ge.11), kind=kOutput, calls=%fused_computation.507 | convolution fusion | flops 33946624 | bytes 823297 | tf_op jit(solution)/shard_map/tid,sd->its/dot_general | solution.py:25
  65.0 32.8 %all-reduce.3.cloned.1.call-done = (bf16[2,256,512]{2,1,0:T(8,128)(2,1)}, bf16[2,256,512]{2,1,0:T(8,128)(2,1)}) async-done(((bf16[2,256,512]{2,1,0:T(8,128)(2,1)}, bf16[2,256,512]{2,1,0:T(8,128)(2,1)}), (bf16[2,256,512]{2,1,0:T(8,128)(2,1)}, bf16[2,256,512]{2,1,0:T(8,128)(2,1)})) %all-reduce.3.cloned.1.call-update) | async-done | bytes 1048592 | tf_op jit(solution)/shard_map/psum | solution.py:14
  97.8 1.3 slice_bitcast_fusion.3
  99.1 0.6 copy-done.19
  100.0 0.3 fusion.342
  100.3 0.7 copy-done.18
  101.2 0.3 fusion.343
  101.9 0.3 fusion.337
  102.5 0.3 fusion.330
  102.8 0.3 copy-done.34
  103.2 0.3 copy-done.32
  103.5 0.3 convolution_bitcast_fusion.22
  104.2 0.4 copy-done.30
  104.6 0.3 convolution_bitcast_fusion.17
  105.3 0.4 copy-done.25
  105.7 0.3 convolution_bitcast_fusion.12
  106.3 0.4 copy-done.22
  106.7 0.9 fusion.106
  107.6 0.3 convolution_bitcast_fusion.7
  108.1 1.0 copy-done.3
  109.5 0.8 copy-done.1
  110.6 0.7 copy-done.4
  111.5 0.4 fusion.152
  111.9 0.8 fusion.104
  113.4 0.4 fusion.67
  114.0 0.3 fusion.71
  115.2 0.6 copy-done.17
  116.4 0.8 copy-done.9
  117.7 0.4 fusion.75
  119.2 0.8 copy-done.8
  120.4 0.4 fusion.79
  121.7 1.3 %copy.105 = bf16[1,128,4096]{2,1,0:T(8,128)(2,1)} copy(bf16[1,128,4096]{1,2,0:T(8,128)(2,1)S(1)} %bitcast.924) | data formatting | bytes 2097152 | tf_op jit(solution)/shard_map/convert_element_type | solution.py:82
  (112 shorter events, 8.8 us)
Async XLA Ops:
  6.5 6.7 %copy-start.15 = (bf16[1,256,512]{2,1,0:T(8,128)(2,1)S(1)}, bf16[1,256,512]{2,1,0:T(8,128)(2,1)}, u32[]{:S(2)}) copy-start(bf16[1,256,512]{2,1,0:T(8,128)(2,1)} %param.11) | copy-start | bytes 786436
  6.5 91.3 %all-reduce.3.cloned.1.call-start = ((), (), s32[]{:S(2)}) async-start(), calls=%async_computation | async-start | bytes 2097152 | tf_op jit(solution)/shard_map/psum | solution.py:14
  7.6 20.9 %collective-permute-start = (bf16[2,128,512]{2,1,0:T(8,128)(2,1)S(1)}, bf16[2,128,512]{2,1,0:T(8,128)(2,1)S(1)}, u32[]{:S(2)}, u32[]{:S(2)}) collective-permute-start(bf16[2,128,512]{2,1,0:T(8,128)(2,1)S(1)} %pad_maximum_fusion.1), channel_id=1, source_target_pairs={{0,1},{1,2},{2,3},{3,4},{4,5},{5,6},{6,7},{7,0},{8,9},{9,10},{10,1... | collective-permute-start | bytes 786440 | tf_op jit(solution)/shard_map/ppermute | solution.py:20
  10.6 0.7 copy-start.36
  13.3 1.0 copy-start.16
  14.2 1.6 %copy-start.12 = (bf16[1,128,4096]{2,1,0:T(8,128)(2,1)S(1)}, bf16[1,128,4096]{2,1,0:T(8,128)(2,1)}, u32[]{:S(2)}) copy-start(bf16[1,128,4096]{2,1,0:T(8,128)(2,1)} %param.8) | copy-start | bytes 3145732
  15.8 0.9 copy-start.13
  20.0 6.7 %copy-start.14 = (bf16[1,128,512]{2,1,0:T(8,128)(2,1)S(1)}, bf16[1,128,512]{2,1,0:T(8,128)(2,1)}, u32[]{:S(2)}) copy-start(bf16[1,128,512]{2,1,0:T(8,128)(2,1)} %param.10) | copy-start | bytes 393220
  21.6 0.7 copy-start.37
  22.9 1.2 copy-start.38
  30.9 12.0 %collective-permute-start.1 = (bf16[2,128,512]{2,1,0:T(8,128)(2,1)S(1)}, bf16[2,128,512]{2,1,0:T(8,128)(2,1)S(1)}, u32[]{:S(2)}, u32[]{:S(2)}) collective-permute-start(bf16[2,128,512]{2,1,0:T(8,128)(2,1)S(1)} %collective-permute-done), channel_id=1, source_target_pairs={{0,1},{1,2},{2,3},{3,4},{4,5},{5,6},{6,7},{7,0},{8,9},{9,10},{10,1... | collective-permute-start | bytes 786440 | tf_op jit(solution)/shard_map/ppermute | solution.py:20
  45.4 12.5 %collective-permute-start.2 = (bf16[2,128,512]{2,1,0:T(8,128)(2,1)S(1)}, bf16[2,128,512]{2,1,0:T(8,128)(2,1)S(1)}, u32[]{:S(2)}, u32[]{:S(2)}) collective-permute-start(bf16[2,128,512]{2,1,0:T(8,128)(2,1)S(1)} %collective-permute-done.1), channel_id=1, source_target_pairs={{0,1},{1,2},{2,3},{3,4},{4,5},{5,6},{6,7},{7,0},{8,9},{9,10},{10,1... | collective-permute-start | bytes 786440 | tf_op jit(solution)/shard_map/ppermute | solution.py:20
  99.1 0.6 copy-start.19
  100.3 0.7 copy-start.18
  102.5 0.7 copy-start.34
  102.5 0.7 copy-start.35
  102.8 0.7 copy-start.32
  102.8 0.7 copy-start.28
  103.5 0.7 copy-start.31
  103.5 0.7 copy-start.33
  103.9 0.7 copy-start.30
  103.9 0.7 copy-start.26
  104.6 0.7 copy-start.27
  104.6 0.7 copy-start.29
  105.0 0.7 copy-start.25
  105.0 0.7 copy-start.20
  105.7 0.7 copy-start.23
  105.7 0.7 copy-start.24
  106.0 0.7 copy-start.22
  106.0 0.7 copy-start.21
  106.7 1.3 copy-start.11
  107.6 1.8 %copy-start.10 = (f32[8,128,128]{1,2,0:T(8,128)S(1)}, f32[8,128,128]{1,2,0:T(8,128)}, u32[]{:S(2)}) copy-start(f32[8,128,128]{1,2,0:T(8,128)} %get-tuple-element.112) | copy-start | bytes 1572868
  107.6 3.0 %copy-start.6 = (f32[8,128,128]{1,2,0:T(8,128)S(1)}, f32[8,128,128]{1,2,0:T(8,128)}, u32[]{:S(2)}) copy-start(f32[8,128,128]{1,2,0:T(8,128)} %get-tuple-element.122) | copy-start | bytes 1572868
  107.6 3.0 %copy-start.7 = (f32[8,128,128]{1,2,0:T(8,128)S(1)}, f32[8,128,128]{1,2,0:T(8,128)}, u32[]{:S(2)}) copy-start(f32[8,128,128]{1,2,0:T(8,128)} %get-tuple-element.110) | copy-start | bytes 1572868
  108.0 1.1 copy-start.3
  108.0 1.3 copy-start.2
  109.3 1.0 copy-start.1
  109.4 1.1 copy-start
  110.3 1.0 copy-start.4
  110.3 1.2 copy-start.5
  114.9 0.9 copy-start.17
  116.1 1.0 copy-start.9
  118.9 1.0 copy-start.8
Sparse Core Ops, SparseCore 0:
  15.5 82.2 all-reduce.2
where the time goes:
time: 131 us; the launch traced here: 130 us
  waiting for transfers between devices  50.9 us (39%)
  matrix products  32.1 us (25%)
  local copies, waits for them, and re-layouts  17.4 us (13%)
  between operations  16.1 us (12%)
  other arithmetic  8.85 us (7%)
  starting transfers between devices  4.57 us (3%)
    psum x1, waiting for transfers between devices, broadcast(): return lax.psum(block, axis)  32.8 us
    dot_general x24, matrix products, merge_block(): jnp.einsum('tid,sd->its', query_rows, key_rows, preferred_element_type=jn...  25.1 us
    ppermute x3, waiting for transfers between devices, from_behind(): return lax.ppermute(value, axis, pairs)  18.1 us
    unnamed x81, local copies, waits for them, and re-layouts  12.8 us
    dot_general x24, matrix products, merge_block(): jnp.einsum('its,sd->itd', weights.astype(jnp.bfloat16), value_rows, prefe...  7.01 us
    ppermute x3, starting transfers between devices, from_behind(): return lax.ppermute(value, axis, pairs)  4.57 us
    reduce_sum x15, other arithmetic, merge_block(): totals = totals * shrink + jnp.sum(weights, axis=-1)  3.35 us
  transfers between devices with their start and end apart: 4, of which 3 were waited for; matrix products, arithmetic and copies ran while one was open for 23% of the time, Pallas kernels for 0%

commit v1 on v0

--- a/solution.py
+++ b/solution.py
@@ -11,7 +11,7 @@
 
 def broadcast(block, axis, source):
     block = jnp.where(lax.axis_index(axis) == source, block, jnp.zeros_like(block))
-    return lax.psum(block, axis)
+    return jnp.sum(lax.all_gather(block, axis), 0)
 
 
 def from_behind(value, axis, steps):

time: 131 us -> 199 us (1.52)
  waiting for transfers between devices: 50.9 us -> 112 us
  local copies, waits for them, and re-layouts: 17.4 us -> 8.65 us
  matrix products: 32.1 us -> 40.2 us
  other arithmetic: 8.85 us -> 16.7 us
    all_gather x0 -> x2, waiting for transfers between devices: none -> 99 us  [broadcast(): return jnp.sum(lax.all_gather(block, axis), 0)]
    psum x1 -> x0, waiting for transfers between devices: 32.8 us -> none  [broadcast(): return lax.psum(block, axis)]
    unnamed x81 -> x92, local copies, waits for them, and re-layouts: 12.8 us -> 2.2 us
    dot_general x24, matrix products: 25.1 us -> 33.2 us  [merge_block(): jnp.einsum('tid,sd->its', query_rows, key_rows, preferred_element_type=jn...]
    reduce_sum x0 -> x2, other arithmetic: none -> 6.68 us  [broadcast(): return jnp.sum(lax.all_gather(block, axis), 0)]
    ppermute x3, waiting for transfers between devices: 18.1 us -> 12 us  [from_behind(): return lax.ppermute(value, axis, pairs)]
    reduce_sum x15 -> x8, other arithmetic: 3.35 us -> 4.11 us  [merge_block(): totals = totals * shrink + jnp.sum(weights, axis=-1)]
  transfers between devices with their start and end apart: 4 -> 5, of which waited for: 3 -> 4; matrix products, arithmetic and copies ran while one was open for 23% -> 20% of each run, Pallas kernels for 0% -> 0%
where the time goes in v1:
time: 199 us; the launch traced here: 198 us
  waiting for transfers between devices  112 us (56%)
  matrix products  40.2 us (20%)
  other arithmetic  16.7 us (8%)
  between operations  16.3 us (8%)
  local copies, waits for them, and re-layouts  8.65 us (4%)
  starting transfers between devices  4.64 us (2%)
    all_gather x2, waiting for transfers between devices, broadcast(): return jnp.sum(lax.all_gather(block, axis), 0)  99 us
    dot_general x24, matrix products, merge_block(): jnp.einsum('tid,sd->its', query_rows, key_rows, preferred_element_type=jn...  33.2 us
    ppermute x3, waiting for transfers between devices, from_behind(): return lax.ppermute(value, axis, pairs)  12 us
    dot_general x24, matrix products, merge_block(): jnp.einsum('its,sd->itd', weights.astype(jnp.bfloat16), value_rows, prefe...  7 us
    reduce_sum x2, other arithmetic, broadcast(): return jnp.sum(lax.all_gather(block, axis), 0)  6.68 us
    ppermute x3, starting transfers between devices, from_behind(): return lax.ppermute(value, axis, pairs)  4.57 us
    reduce_sum x8, other arithmetic, merge_block(): totals = totals * shrink + jnp.sum(weights, axis=-1)  4.11 us
  transfers between devices with their start and end apart: 5, of which 4 were waited for; matrix products, arithmetic and copies ran while one was open for 20% of the time, Pallas kernels for 0%

profile of v1, /device:TPU:0, one launch (start us, length us, event | category | flops | bytes accessed | tf_op | source)
XLA Modules:
  0.0 198.2 jit_solution(13344420917345412719)
XLA Ops:
  6.6 1.4 fusion.325
  9.3 2.1 %broadcast_select_fusion.1 = (bf16[1,2,256,512]{3,2,1,0:T(8,128)(2,1)}, bf16[1,2,256,512]{3,2,1,0:T(8,128)(2,1)}) fusion(pred[]{:T(512)S(6)} %eq.14, bf16[1,1,256,512]{3,2,1,0:T(8,128)(2,1)} %bitcast.935, bf16[1,1,256,512]{3,2,1,0:T(8,128)(2,1)} %bitcast.936, pred[]{:T(512)S(6)} %eq.15), kind=kLoop, calls=%fused_computation.219 | loop fusion | flops 786432 | bytes 1572866 | tf_op jit(solution)/shard_map/jit(_where)/select_n | solution.py:13
  11.5 0.7 all-gather.3.cloned.1.call-update
  12.2 1.0 pad_maximum_fusion.2
  13.2 3.0 %collective-permute-start = (bf16[2,128,512]{2,1,0:T(8,128)(2,1)S(1)}, bf16[2,128,512]{2,1,0:T(8,128)(2,1)S(1)}, u32[]{:S(2)}, u32[]{:S(2)}) collective-permute-start(bf16[2,128,512]{2,1,0:T(8,128)(2,1)S(1)} %pad_maximum_fusion.2), channel_id=1, source_target_pairs={{0,1},{1,2},{2,3},{3,4},{4,5},{5,6},{6,7},{7,0},{8,9},{9,10},{10,1... | collective-permute-start | bytes 786440 | tf_op jit(solution)/shard_map/ppermute | solution.py:20
  16.2 1.6 copy.106
  17.8 0.6 fusion.326
  18.5 0.6 iota_compare_fusion.1
  19.1 0.6 fusion.284
  19.8 1.7 fusion.338
  21.4 1.7 fusion.344
  23.1 1.6 fusion.350
  24.7 1.3 iota_compare_fusion.2
  26.7 1.6 fusion.332
  28.3 1.5 collective-permute-start.1
  29.9 0.7 slice_bitcast_fusion.12
  30.6 1.6 fusion.335
  32.2 1.7 fusion.341
  33.8 1.6 fusion.347
  35.4 1.6 fusion.329
  37.1 8.3 %collective-permute-done.1 = bf16[2,128,512]{2,1,0:T(8,128)(2,1)S(1)} collective-permute-done((bf16[2,128,512]{2,1,0:T(8,128)(2,1)S(1)}, bf16[2,128,512]{2,1,0:T(8,128)(2,1)S(1)}, u32[]{:S(2)}, u32[]{:S(2)}) %collective-permute-start.1) | collective-permute-done | bytes 262176 | tf_op jit(solution)/shard_map/ppermute | solution.py:20
  45.4 0.7 slice_bitcast_fusion.10
  46.1 1.6 fusion.334
  47.7 1.6 fusion.340
  49.3 1.6 fusion.346
  50.9 1.6 fusion.328
  52.5 3.7 %collective-permute-done.2 = bf16[2,128,512]{2,1,0:T(8,128)(2,1)S(1)} collective-permute-done((bf16[2,128,512]{2,1,0:T(8,128)(2,1)S(1)}, bf16[2,128,512]{2,1,0:T(8,128)(2,1)S(1)}, u32[]{:S(2)}, u32[]{:S(2)}) %collective-permute-start.2) | collective-permute-done | bytes 262176 | tf_op jit(solution)/shard_map/ppermute | solution.py:20
  56.2 0.7 slice_bitcast_fusion.8
  56.9 1.6 fusion.333
  58.5 1.6 fusion.339
  60.1 1.6 fusion.345
  61.7 1.6 fusion.327
  63.3 29.8 %all-gather.5.cloned.1.call-done = bf16[8,2,256,512]{3,2,1,0:T(8,128)(2,1)} async-done(((bf16[1,2,256,512]{3,2,1,0:T(8,128)(2,1)}), bf16[8,2,256,512]{3,2,1,0:T(8,128)(2,1)}) %all-gather.5.cloned.1.call-update) | async-done | bytes 4194320 | tf_op jit(solution)/shard_map/all_gather | solution.py:14
  93.1 3.0 %reduce_sum.298 = bf16[2,256,512]{2,1,0:T(8,128)(2,1)S(1)} reduce(bf16[8,2,256,512]{3,2,1,0:T(8,128)(2,1)} %all-gather.5.cloned.1.call-done, bf16[]{:T(256)} %constant.60.clone.1), dimensions={0}, to_apply=%region_3.4 | reduce | flops 1835008 | bytes 4718594 | tf_op jit(solution)/shard_map/reduce_sum | solution.py:14
  96.1 0.9 fusion.336
  97.0 1.5 fusion.342
  98.5 69.1 %all-gather.3.cloned.1.call-done = bf16[8,2,256,512]{3,2,1,0:T(8,128)(2,1)} async-done(((bf16[1,2,256,512]{3,2,1,0:T(8,128)(2,1)}), bf16[8,2,256,512]{3,2,1,0:T(8,128)(2,1)}) %all-gather.3.cloned.1.call-update) | async-done | bytes 4194320 | tf_op jit(solution)/shard_map/all_gather | solution.py:14
  167.7 3.7 %reduce_sum.297 = bf16[2,256,512]{2,1,0:T(8,128)(2,1)} reduce(bf16[8,2,256,512]{3,2,1,0:T(8,128)(2,1)} %all-gather.3.cloned.1.call-done, bf16[]{:T(256)} %constant.60.clone.1), dimensions={0}, to_apply=%region_1.2 | reduce | flops 1835008 | bytes 4718594 | tf_op jit(solution)/shard_map/reduce_sum | solution.py:14
  171.4 1.1 slice_bitcast_fusion.5
  172.5 1.0 fusion.337
  173.5 1.0 fusion.343
  174.5 1.1 fusion.348
  175.7 0.3 fusion.349
  176.0 0.3 fusion.331
  176.4 1.2 fusion.330
  177.7 0.3 convolution_bitcast_fusion.22
  178.2 0.3 convolution_bitcast_fusion.17
  178.6 0.3 convolution_bitcast_fusion.12
  179.0 0.3 convolution_bitcast_fusion.7
  180.0 0.4 fusion.152
  180.5 2.5 %fusion.104 = (f32[8,128]{1,0:T(8,128)S(1)}, f32[8,128]{1,0:T(8,128)S(1)}, f32[8,128]{1,0:T(8,128)S(1)}, f32[8,128]{1,0:T(8,128)S(1)}, f32[8,128]{1,0:T(8,128)S(...) fusion(f32[8,128,256]{1,2,0:T(8,128)S(1)} %get-tuple-element.106, ...), kind=kLoop, calls=%fused_computation.161 | loop fusion | flops 6283264 | bytes 8454656 | tf_op jit(solution)/shard_map/reduce_sum | solution.py:32
  183.6 0.4 fusion.67
  183.9 0.3 fusion.80
  184.2 0.4 fusion.71
  184.6 0.3 fusion.83
  184.9 0.3 fusion.81
  185.2 0.3 fusion.84
  185.5 0.3 fusion.100
  185.8 0.3 fusion.101
  187.2 0.4 fusion.75
  188.2 0.3 fusion.102
  188.7 0.4 fusion.79
  189.6 0.3 fusion.103
  190.1 1.3 copy.156
  (121 shorter events, 4.3 us)
Async XLA Ops:
  6.5 20.0 %copy-start.20 = (bf16[1,128,512]{2,1,0:T(8,128)(2,1)S(1)}, bf16[1,128,512]{2,1,0:T(8,128)(2,1)}, u32[]{:S(2)}) copy-start(bf16[1,128,512]{2,1,0:T(8,128)(2,1)} %param.10) | copy-start | bytes 393220
  6.5 13.2 %copy-start.17 = (bf16[1,128,512]{2,1,0:T(8,128)(2,1)S(1)}, bf16[1,128,512]{2,1,0:T(8,128)(2,1)}, u32[]{:S(2)}) copy-start(bf16[1,128,512]{2,1,0:T(8,128)(2,1)} %param.9) | copy-start | bytes 393220
  6.5 11.3 %copy-start.43 = (s32[2]{0:T(128)S(1)}, s32[2]{0:T(128)}, u32[]{:S(2)}) copy-start(s32[2]{0:T(128)} %param.13) | copy-start | bytes 28
  6.5 12.6 %copy-start.44 = (s32[2]{0:T(128)S(1)}, s32[2]{0:T(128)}, u32[]{:S(2)}) copy-start(s32[2]{0:T(128)} %param.15) | copy-start | bytes 28
  6.5 86.6 %all-gather.5.cloned.1.call-start = ((), (), s32[]{:S(2)}) async-start(), calls=%async_computation.1 | async-start | bytes 4718592 | tf_op jit(solution)/shard_map/all_gather | solution.py:14
  11.4 156.2 %all-gather.3.cloned.1.call-start = ((), (), s32[]{:S(2)}) async-start(), calls=%async_computation | async-start | bytes 4718592 | tf_op jit(solution)/shard_map/all_gather | solution.py:14
  13.2 15.1 %collective-permute-start = (bf16[2,128,512]{2,1,0:T(8,128)(2,1)S(1)}, bf16[2,128,512]{2,1,0:T(8,128)(2,1)S(1)}, u32[]{:S(2)}, u32[]{:S(2)}) collective-permute-start(bf16[2,128,512]{2,1,0:T(8,128)(2,1)S(1)} %pad_maximum_fusion.2), channel_id=1, source_target_pairs={{0,1},{1,2},{2,3},{3,4},{4,5},{5,6},{6,7},{7,0},{8,9},{9,10},{10,1... | collective-permute-start | bytes 786440 | tf_op jit(solution)/shard_map/ppermute | solution.py:20
  19.1 77.0 %copy-start.23 = (pred[256]{0:T(512)(128)(4,1)}, pred[256]{0:T(512)(128)(4,1)S(1)}, u32[]{:S(2)}) copy-start(pred[256]{0:T(512)(128)(4,1)S(1)} %iota_compare_fusion.1) | copy-start | bytes 772
  28.3 17.1 %collective-permute-start.1 = (bf16[2,128,512]{2,1,0:T(8,128)(2,1)S(1)}, bf16[2,128,512]{2,1,0:T(8,128)(2,1)S(1)}, u32[]{:S(2)}, u32[]{:S(2)}) collective-permute-start(bf16[2,128,512]{2,1,0:T(8,128)(2,1)S(1)} %collective-permute-done), channel_id=1, source_target_pairs={{0,1},{1,2},{2,3},{3,4},{4,5},{5,6},{6,7},{7,0},{8,9},{9,10},{10,1... | collective-permute-start | bytes 786440 | tf_op jit(solution)/shard_map/ppermute | solution.py:20
  45.4 10.8 %collective-permute-start.2 = (bf16[2,128,512]{2,1,0:T(8,128)(2,1)S(1)}, bf16[2,128,512]{2,1,0:T(8,128)(2,1)S(1)}, u32[]{:S(2)}, u32[]{:S(2)}) collective-permute-start(bf16[2,128,512]{2,1,0:T(8,128)(2,1)S(1)} %collective-permute-done.1), channel_id=1, source_target_pairs={{0,1},{1,2},{2,3},{3,4},{4,5},{5,6},{6,7},{7,0},{8,9},{9,10},{10,1... | collective-permute-start | bytes 786440 | tf_op jit(solution)/shard_map/ppermute | solution.py:20
  96.1 0.9 copy-start.16
  171.4 4.3 %copy-start.22 = (pred[256]{0:T(512)(128)(4,1)S(1)}, pred[256]{0:T(512)(128)(4,1)}, u32[]{:S(2)}) copy-start(pred[256]{0:T(512)(128)(4,1)} %iota_compare_fusion.2) | copy-start | bytes 772
  171.4 4.9 %copy-start.24 = (pred[256]{0:T(512)(128)(4,1)S(1)}, pred[256]{0:T(512)(128)(4,1)}, u32[]{:S(2)}) copy-start(pred[256]{0:T(512)(128)(4,1)} %copy-done.23) | copy-start | bytes 772
  172.5 5.2 %copy-start.34 = (f32[8,128]{1,0:T(8,128)S(1)}, f32[8,128]{1,0:T(8,128)}, u32[]{:S(2)}) copy-start(f32[8,128]{1,0:T(8,128)} %get-tuple-element.107) | copy-start | bytes 12292
  172.5 5.2 %copy-start.37 = (f32[8,128]{1,0:T(8,128)S(1)}, f32[8,128]{1,0:T(8,128)}, u32[]{:S(2)}) copy-start(f32[8,128]{1,0:T(8,128)} %get-tuple-element.101) | copy-start | bytes 12292
  172.5 5.2 %copy-start.39 = (f32[8,128]{1,0:T(8,128)S(1)}, f32[8,128]{1,0:T(8,128)}, u32[]{:S(2)}) copy-start(f32[8,128]{1,0:T(8,128)} %get-tuple-element.99) | copy-start | bytes 12292
  172.5 5.2 %copy-start.41 = (f32[8,128]{1,0:T(8,128)S(1)}, f32[8,128]{1,0:T(8,128)}, u32[]{:S(2)}) copy-start(f32[8,128]{1,0:T(8,128)} %get-tuple-element.97) | copy-start | bytes 12292
  172.5 5.2 %copy-start.42 = (f32[8,128]{1,0:T(8,128)S(1)}, f32[8,128]{1,0:T(8,128)}, u32[]{:S(2)}) copy-start(f32[8,128]{1,0:T(8,128)} %get-tuple-element.103) | copy-start | bytes 12292
  173.5 4.6 %copy-start.32 = (f32[8,128]{1,0:T(8,128)S(1)}, f32[8,128]{1,0:T(8,128)}, u32[]{:S(2)}) copy-start(f32[8,128]{1,0:T(8,128)} %get-tuple-element.119) | copy-start | bytes 12292
  173.5 4.6 %copy-start.35 = (f32[8,128]{1,0:T(8,128)S(1)}, f32[8,128]{1,0:T(8,128)}, u32[]{:S(2)}) copy-start(f32[8,128]{1,0:T(8,128)} %get-tuple-element.113) | copy-start | bytes 12292
  173.5 4.6 %copy-start.36 = (f32[8,128]{1,0:T(8,128)S(1)}, f32[8,128]{1,0:T(8,128)}, u32[]{:S(2)}) copy-start(f32[8,128]{1,0:T(8,128)} %get-tuple-element.111) | copy-start | bytes 12292
  173.5 4.6 %copy-start.38 = (f32[8,128]{1,0:T(8,128)S(1)}, f32[8,128]{1,0:T(8,128)}, u32[]{:S(2)}) copy-start(f32[8,128]{1,0:T(8,128)} %get-tuple-element.109) | copy-start | bytes 12292
  173.5 4.6 %copy-start.40 = (f32[8,128]{1,0:T(8,128)S(1)}, f32[8,128]{1,0:T(8,128)}, u32[]{:S(2)}) copy-start(f32[8,128]{1,0:T(8,128)} %get-tuple-element.115) | copy-start | bytes 12292
  174.5 4.0 %copy-start.26 = (f32[8,128]{1,0:T(8,128)S(1)}, f32[8,128]{1,0:T(8,128)}, u32[]{:S(2)}) copy-start(f32[8,128]{1,0:T(8,128)} %get-tuple-element.131) | copy-start | bytes 12292
  174.5 4.0 %copy-start.30 = (f32[8,128]{1,0:T(8,128)S(1)}, f32[8,128]{1,0:T(8,128)}, u32[]{:S(2)}) copy-start(f32[8,128]{1,0:T(8,128)} %get-tuple-element.125) | copy-start | bytes 12292
  174.5 4.0 %copy-start.31 = (f32[8,128]{1,0:T(8,128)S(1)}, f32[8,128]{1,0:T(8,128)}, u32[]{:S(2)}) copy-start(f32[8,128]{1,0:T(8,128)} %get-tuple-element.123) | copy-start | bytes 12292
  174.5 4.0 %copy-start.33 = (f32[8,128]{1,0:T(8,128)S(1)}, f32[8,128]{1,0:T(8,128)}, u32[]{:S(2)}) copy-start(f32[8,128]{1,0:T(8,128)} %get-tuple-element.121) | copy-start | bytes 12292
  176.0 2.9 %copy-start.25 = (f32[8,128]{1,0:T(8,128)S(1)}, f32[8,128]{1,0:T(8,128)}, u32[]{:S(2)}) copy-start(f32[8,128]{1,0:T(8,128)} %get-tuple-element.95) | copy-start | bytes 12292
  176.0 2.9 %copy-start.27 = (f32[8,128]{1,0:T(8,128)S(1)}, f32[8,128]{1,0:T(8,128)}, u32[]{:S(2)}) copy-start(f32[8,128]{1,0:T(8,128)} %get-tuple-element.89) | copy-start | bytes 12292
  176.0 2.9 %copy-start.28 = (f32[8,128]{1,0:T(8,128)S(1)}, f32[8,128]{1,0:T(8,128)}, u32[]{:S(2)}) copy-start(f32[8,128]{1,0:T(8,128)} %get-tuple-element.87) | copy-start | bytes 12292
  176.0 2.9 %copy-start.29 = (f32[8,128]{1,0:T(8,128)S(1)}, f32[8,128]{1,0:T(8,128)}, u32[]{:S(2)}) copy-start(f32[8,128]{1,0:T(8,128)} %get-tuple-element.85) | copy-start | bytes 12292
  176.4 3.0 %copy-start.8 = (f32[8,128,128]{1,2,0:T(8,128)S(1)}, f32[8,128,128]{1,2,0:T(8,128)}, u32[]{:S(2)}) copy-start(f32[8,128,128]{1,2,0:T(8,128)} %get-tuple-element.114) | copy-start | bytes 1572868
  176.4 3.0 %copy-start.9 = (f32[8,128,128]{1,2,0:T(8,128)S(1)}, f32[8,128,128]{1,2,0:T(8,128)}, u32[]{:S(2)}) copy-start(f32[8,128,128]{1,2,0:T(8,128)} %get-tuple-element.102) | copy-start | bytes 1572868
  177.6 1.9 copy-start.10
  177.6 1.9 copy-start.11
  177.7 2.1 %copy-start.14 = (f32[8,128,128]{1,2,0:T(8,128)S(1)}, f32[8,128,128]{1,2,0:T(8,128)}, u32[]{:S(2)}) copy-start(f32[8,128,128]{1,2,0:T(8,128)} %get-tuple-element.110) | copy-start | bytes 1572868
  177.7 2.1 %copy-start.15 = (f32[8,128,128]{1,2,0:T(8,128)S(1)}, f32[8,128,128]{1,2,0:T(8,128)}, u32[]{:S(2)}) copy-start(f32[8,128,128]{1,2,0:T(8,128)} %get-tuple-element.98) | copy-start | bytes 1572868
  178.0 1.9 copy-start
  178.1 1.9 copy-start.2
  178.1 1.9 copy-start.6
  178.1 1.9 copy-start.7
  183.0 1.0 copy-start.18
  183.5 1.3 copy-start.19
  183.9 1.6 copy-start.21
  184.9 1.2 copy-start.1
  184.9 1.2 copy-start.4
  185.2 1.1 copy-start.3
  185.2 1.3 copy-start.5
  185.2 1.5 copy-start.12
  185.2 1.6 copy-start.13
Sparse Core Ops, SparseCore 0:
  11.6 81.5 all-gather.4
  95.2 72.3 all-gather.2
